TPU v7x, 32 devices: a whole 2x2x4 slice. The times are simulated.
32 devices in a mesh: row: 8 (over y, x, core), col: 4 (over z).
Axes of the slice: x: 2, y: 2, z: 4, core: 2. Of those that a mesh axis runs over, the one named last changes fastest.
Arguments:
- pair: bfloat16 [64, 64, 128], P('row', 'col'), may hold values from -6 to 6
- pair_mask: int32 [64, 64], P('row', 'col'), may hold values 0 or 1
- ln_in_gain: float32 [128], replicated, may hold values from 0.1 to 1.9
- ln_in_bias: float32 [128], replicated, may hold values from -3 to 3
- w_proj: bfloat16 [128, 512], replicated, may hold values from -0.5 to 0.5
- b_proj: float32 [512], replicated, may hold values from -3 to 3
- w_gate: bfloat16 [128, 128], replicated, may hold values from -0.5 to 0.5
- b_gate: float32 [128], replicated, may hold values from -3 to 3
- ln_mid_gain: float32 [128], replicated, may hold values from 0.1 to 1.9
- ln_mid_bias: float32 [128], replicated, may hold values from -3 to 3
- w_out: bfloat16 [128, 128], replicated, may hold values from -0.5 to 0.5
- b_out: float32 [128], replicated, may hold values from -3 to 3
- cotangent: bfloat16 [64, 64, 128], P('row', 'col'), may hold values from -6 to 6
Outputs:
- update: bfloat16 [64, 64, 128], P('row', 'col')
- pair_grad: float32 [64, 64, 128], P('row', 'col')
All inputs are finite; a program needn't handle non-finite values. No bound on the sum of `pair_mask` on one device may be relied on, other than what follows from the above.
Results may differ from a plain program's by a relative error of at most 0.019.
Values may be sent and summed in bfloat16 or wider, within the bound.
A program may use at most 64 MiB of HBM per device.

v0:
```python
import jax
import jax.numpy as jnp
from jax import lax
from jax.sharding import PartitionSpec as P


def layer_norm(values, gain_vec, bias_vec):
    average = jnp.mean(values, -1, keepdims=True)
    centred = values - average
    inv_std = lax.rsqrt(jnp.mean(centred * centred, -1, keepdims=True) + 1e-05)
    hat_val = centred * inv_std
    return (hat_val * gain_vec + bias_vec, hat_val, inv_std)


def norm_back(upstream, hat_val, inv_std, gain_vec):
    scaled = upstream * gain_vec
    return inv_std * (
        scaled
        - jnp.mean(scaled, -1, keepdims=True)
        - hat_val * jnp.mean(scaled * hat_val, -1, keepdims=True)
    )


def gate_pair(proj, mask_f):
    hidden = proj.shape[-1] // 4
    sig_a = jax.nn.sigmoid(proj[..., :hidden])
    sig_b = jax.nn.sigmoid(proj[..., 2 * hidden : 3 * hidden])
    a_bf = (mask_f * sig_a * proj[..., hidden : 2 * hidden]).astype(jnp.bfloat16)
    b_bf = (mask_f * sig_b * proj[..., 3 * hidden :]).astype(jnp.bfloat16)
    return (a_bf, b_bf)


def gate_back(grad_a, grad_b, proj, mask_f):
    hidden = proj.shape[-1] // 4
    sig_a = jax.nn.sigmoid(proj[..., :hidden])
    val_a = proj[..., hidden : 2 * hidden]
    sig_b = jax.nn.sigmoid(proj[..., 2 * hidden : 3 * hidden])
    val_b = proj[..., 3 * hidden :]
    masked_a = grad_a * mask_f
    masked_b = grad_b * mask_f
    return jnp.concatenate(
        [
            masked_a * val_a * sig_a * (1.0 - sig_a),
            masked_a * sig_a,
            masked_b * val_b * sig_b * (1.0 - sig_b),
            masked_b * sig_b,
        ],
        -1,
    )


def per_device(
    pair,
    pair_mask,
    ln_in_gain,
    ln_in_bias,
    w_proj,
    b_proj,
    w_gate,
    b_gate,
    ln_mid_gain,
    ln_mid_bias,
    w_out,
    b_out,
    cotangent,
):
    normed, hat_in, rstd_in = layer_norm(pair.astype(jnp.float32), ln_in_gain, ln_in_bias)
    x_bf = normed.astype(jnp.bfloat16)
    proj = jnp.dot(x_bf, w_proj, preferred_element_type=jnp.float32) + b_proj
    mask_f = pair_mask.astype(jnp.float32)[..., None]
    a_bf, b_bf = gate_pair(proj, mask_f)
    b_every = lax.all_gather(b_bf, "row", axis=0, tiled=True)
    owned = lax.psum_scatter(
        jnp.einsum("jkh,ikh->jih", b_every, a_bf, preferred_element_type=jnp.float32).astype(
            jnp.bfloat16
        ),
        "col",
        scatter_dimension=0,
        tiled=True,
    ).astype(jnp.float32)
    triangle = jnp.transpose(owned, (1, 0, 2))
    mid_val, hat_mid, rstd_mid = layer_norm(triangle, ln_mid_gain, ln_mid_bias)
    mid_bf = mid_val.astype(jnp.bfloat16)
    out_lin = jnp.dot(mid_bf, w_out, preferred_element_type=jnp.float32) + b_out
    gate = jax.nn.sigmoid(jnp.dot(x_bf, w_gate, preferred_element_type=jnp.float32) + b_gate)
    update = (gate * out_lin).astype(jnp.bfloat16)
    grad_out = cotangent.astype(jnp.float32)
    d_out = (grad_out * gate).astype(jnp.bfloat16)
    d_gpre = (grad_out * out_lin * gate * (1.0 - gate)).astype(jnp.bfloat16)
    d_mid = jnp.dot(d_out, w_out.T, preferred_element_type=jnp.float32)
    d_tri = norm_back(d_mid, hat_mid, rstd_mid, ln_mid_gain).astype(jnp.bfloat16)
    tri_rows = lax.all_gather(d_tri, "col", axis=1, tiled=True)
    grad_a = jnp.einsum("ijh,jkh->ikh", tri_rows, b_every, preferred_element_type=jnp.float32)
    grad_b = lax.psum_scatter(
        jnp.einsum("ijh,ikh->jkh", tri_rows, a_bf, preferred_element_type=jnp.float32).astype(
            jnp.bfloat16
        ),
        "row",
        scatter_dimension=0,
        tiled=True,
    ).astype(jnp.float32)
    d_proj = gate_back(grad_a, grad_b, proj, mask_f).astype(jnp.bfloat16)
    d_x = jnp.dot(d_proj, w_proj.T, preferred_element_type=jnp.float32) + jnp.dot(
        d_gpre, w_gate.T, preferred_element_type=jnp.float32
    )
    pair_grad = norm_back(d_x, hat_in, rstd_in, ln_in_gain)
    return (update, pair_grad)


def solution(mesh):
    placed = (
        P("row", "col", None),
        P("row", "col"),
        P(),
        P(),
        P(),
        P(),
        P(),
        P(),
        P(),
        P(),
        P(),
        P(),
        P("row", "col", None),
    )
    return jax.shard_map(
        per_device,
        mesh=mesh,
        in_specs=placed,
        out_specs=(P("row", "col", None), P("row", "col", None)),
        check_vma=False,
    )
```

profile of v0, /device:TPU:0, one launch (start us, length us, event | category | flops | bytes accessed | tf_op | source)
XLA Modules:
  0.0 108.7 jit_solution(9767718973377871491)
XLA Ops:
  7.2 0.0 copy-start
  7.2 0.0 reduce-scatter.3.cloned.1.call-start
  7.2 0.7 convert_element_type.52
  7.9 0.8 convert_reduce_fusion
  8.8 0.9 fusion.26
  9.8 1.0 convolution_add_fusion
  10.8 0.1 multiply_convert_fusion.5
  10.9 10.8 %all_gather.6 = bf16[64,16,128]{2,1,0:T(8,128)(2,1)S(1)} all-gather(bf16[8,16,128]{2,1,0:T(8,128)(2,1)S(1)} %get-tuple-element.12), channel_id=1, replica_groups=mesh['row'=8,'col'=4] {'row'}, dimensions={0}, use_global_device_ids=true | all-gather | bytes 294912 | tf_op jit(solution)/shard_map/all_gather | solution.py:72
  21.6 0.2 copy.23
  21.8 3.0 %copy.24 = bf16[64,16,128]{1,0,2:T(8,128)(2,1)S(1)} copy(bf16[64,16,128]{2,1,0:T(8,128)(2,1)S(1)} %all_gather.6) | data formatting | bytes 524288 | tf_op jit(solution)/shard_map/all_gather | solution.py:72
  24.8 0.0 copy-start.9
  24.8 0.0 copy-start.14
  24.8 0.0 copy-start.15
  24.8 0.0 copy-start.16
  24.8 0.0 copy-start.1
  24.9 0.0 copy-start.10
  24.9 0.0 copy-start.12
  24.9 0.0 copy-start.13
  24.9 0.0 copy-start.17
  24.9 0.0 copy-start.5
  24.9 1.2 %fusion = bf16[64,8,128]{0,1,2:T(8,128)(2,1)S(1)} fusion(bf16[8,16,128]{1,0,2:T(8,128)(2,1)S(1)} %copy.23, bf16[64,16,128]{1,0,2:T(8,128)(2,1)S(1)} %copy.24), kind=kOutput, calls=%fused_computation.1 | convolution fusion | flops 2162688 | bytes 425984 | tf_op jit(solution)/shard_map/jkh,ikh->jih/dot_general | solution.py:74
  26.1 0.9 copy.25
  27.0 0.0 reduce-scatter.3.cloned.1.call-update
  27.0 0.0 reduce-scatter.5.cloned.1.call-start
  27.0 19.6 %reduce-scatter.3.cloned.1.call-done = bf16[16,8,128]{2,1,0:T(8,128)(2,1)} async-done(((bf16[64,8,128]{2,1,0:T(8,128)(2,1)}), bf16[16,8,128]{2,1,0:T(8,128)(2,1)}) %reduce-scatter.3.cloned.1.call-update) | async-done | bytes 32784 | tf_op jit(solution)/shard_map/reduce_scatter | solution.py:73
  46.7 0.8 bitcast_reduce_fusion
  47.5 0.9 fusion.48
  48.5 1.0 convolution_add_fusion.2
  49.5 0.0 copy-done.10
  49.5 0.9 multiply_convert_fusion.4
  50.4 1.0 fusion.67
  51.4 0.9 fusion.47
  52.4 13.4 %all_gather.7 = bf16[8,64,128]{2,0,1:T(8,128)(2,1)S(1)} all-gather(bf16[8,16,128]{2,0,1:T(8,128)(2,1)S(1)} %copy.27), channel_id=1, replica_groups=mesh['row'=8,'col'=4] {'col'}, dimensions={1}, use_global_device_ids=true | all-gather | bytes 163840 | tf_op jit(solution)/shard_map/all_gather | solution.py:92
  65.8 0.2 copy.29
  66.0 0.4 fusion.69
  66.4 1.3 %copy.33 = bf16[128,16,64]{0,1,2:T(8,128)(2,1)} copy(bf16[128,16,64]{2,1,0:T(8,128)(2,1)S(1)} %fusion.69) | data formatting | bytes 524288 | tf_op jit(solution)/shard_map/ijh,ikh->jkh/dot_general | solution.py:95
  67.7 0.0 reduce-scatter.5.cloned.1.call-update
  67.7 0.0 copy-start.2
  67.7 0.0 copy-start.4
  67.7 0.0 copy-start.6
  67.7 0.0 copy-start.11
  67.7 0.7 fusion.68
  68.4 0.2 copy.30
  68.6 31.1 %reduce-scatter.5.cloned.1.call-done = bf16[8,16,128]{2,1,0:T(8,128)(2,1)} async-done(((bf16[64,16,128]{2,1,0:T(8,128)(2,1)}), bf16[8,16,128]{2,1,0:T(8,128)(2,1)}) %reduce-scatter.5.cloned.1.call-update) | async-done | bytes 32784 | tf_op jit(solution)/shard_map/reduce_scatter | solution.py:94
  99.7 0.9 multiply_convert_fusion.3
  100.5 0.2 fusion.6
  100.8 0.3 fusion.66
  101.1 0.8 fusion.25
  (28 shorter events, 0.1 us)
Async XLA Ops:
  7.2 2.6 %copy-start = (bf16[128,512]{1,0:T(8,128)(2,1)S(1)}, bf16[128,512]{1,0:T(8,128)(2,1)}, u32[]{:S(2)}) copy-start(bf16[128,512]{1,0:T(8,128)(2,1)} %param.17) | copy-start | bytes 393220
  7.2 39.5 %reduce-scatter.3.cloned.1.call-start = ((), (), s32[]{:S(2)}) async-start(), calls=%async_computation.2 | async-start | bytes 163840 | tf_op jit(solution)/shard_map/reduce_scatter | solution.py:73
  24.8 23.7 %copy-start.9 = (bf16[128,128]{1,0:T(8,128)(2,1)S(1)}, bf16[128,128]{1,0:T(8,128)(2,1)}, u32[]{:S(2)}) copy-start(bf16[128,128]{1,0:T(8,128)(2,1)} %param.23) | copy-start | bytes 98308
  24.8 23.7 %copy-start.14 = (f32[128]{0:T(128)S(1)}, f32[128]{0:T(128)}, u32[]{:S(2)}) copy-start(f32[128]{0:T(128)} %param.21) | copy-start | bytes 1540
  24.8 23.7 %copy-start.15 = (f32[128]{0:T(128)S(1)}, f32[128]{0:T(128)}, u32[]{:S(2)}) copy-start(f32[128]{0:T(128)} %param.24) | copy-start | bytes 1540
  24.8 23.7 %copy-start.16 = (f32[128]{0:T(128)S(1)}, f32[128]{0:T(128)}, u32[]{:S(2)}) copy-start(f32[128]{0:T(128)} %param.22) | copy-start | bytes 1540
  24.8 24.6 %copy-start.1 = (bf16[8,16,128]{2,1,0:T(8,128)(2,1)S(1)}, bf16[8,16,128]{2,1,0:T(8,128)(2,1)}, u32[]{:S(2)}) copy-start(bf16[8,16,128]{2,1,0:T(8,128)(2,1)} %param.13) | copy-start | bytes 98308
  24.9 24.6 %copy-start.10 = (bf16[128,128]{1,0:T(8,128)(2,1)S(1)}, bf16[128,128]{1,0:T(8,128)(2,1)}, u32[]{:S(2)}) copy-start(bf16[128,128]{1,0:T(8,128)(2,1)} %param.19) | copy-start | bytes 98308
  24.9 24.6 %copy-start.12 = (f32[128]{0:T(128)S(1)}, f32[128]{0:T(128)}, u32[]{:S(2)}) copy-start(f32[128]{0:T(128)} %param.15) | copy-start | bytes 1540
  24.9 24.6 %copy-start.13 = (f32[128]{0:T(128)S(1)}, f32[128]{0:T(128)}, u32[]{:S(2)}) copy-start(f32[128]{0:T(128)} %param.16) | copy-start | bytes 1540
  24.9 24.6 %copy-start.17 = (f32[128]{0:T(128)S(1)}, f32[128]{0:T(128)}, u32[]{:S(2)}) copy-start(f32[128]{0:T(128)} %param.20) | copy-start | bytes 1540
  24.9 25.5 %copy-start.5 = (bf16[8,16,128]{2,1,0:T(8,128)(2,1)S(1)}, bf16[8,16,128]{2,1,0:T(8,128)(2,1)}, u32[]{:S(2)}) copy-start(bf16[8,16,128]{2,1,0:T(8,128)(2,1)} %param.25) | copy-start | bytes 98308
  27.0 72.7 %reduce-scatter.5.cloned.1.call-start = ((), (), s32[]{:S(2)}) async-start(), calls=%async_computation.3 | async-start | bytes 294912 | tf_op jit(solution)/shard_map/reduce_scatter | solution.py:94
  49.5 0.9 copy-start.7
  50.4 2.0 %copy-start.3 = (f32[8,16,128]{2,1,0:T(8,128)}, f32[8,16,128]{2,1,0:T(8,128)S(1)}, u32[]{:S(2)}) copy-start(f32[8,16,128]{2,1,0:T(8,128)S(1)} %get-tuple-element.15) | copy-start | bytes 196612
  67.7 33.0 %copy-start.2 = (bf16[8,16,128]{2,1,0:T(8,128)(2,1)S(1)}, bf16[8,16,128]{2,1,0:T(8,128)(2,1)}, u32[]{:S(2)}) copy-start(bf16[8,16,128]{2,1,0:T(8,128)(2,1)} %param.13) | copy-start | bytes 98308
  67.7 33.0 %copy-start.4 = (f32[8,16,128]{2,1,0:T(8,128)S(1)}, f32[8,16,128]{2,1,0:T(8,128)}, u32[]{:S(2)}) copy-start(f32[8,16,128]{2,1,0:T(8,128)} %copy-done.3) | copy-start | bytes 196612
  67.7 33.0 %copy-start.6 = (bf16[8,16,128]{2,1,0:T(8,128)(2,1)S(1)}, bf16[8,16,128]{2,1,0:T(8,128)(2,1)}, u32[]{:S(2)}) copy-start(bf16[8,16,128]{2,1,0:T(8,128)(2,1)} %param.25) | copy-start | bytes 98308
  67.7 33.0 %copy-start.8 = (f32[8,16,128]{2,1,0:T(8,128)S(1)}, f32[8,16,128]{2,1,0:T(8,128)}, u32[]{:S(2)}) copy-start(f32[8,16,128]{2,1,0:T(8,128)} %copy-done.7) | copy-start | bytes 196612
  67.7 33.0 %copy-start.11 = (bf16[128,128]{1,0:T(8,128)(2,1)S(1)}, bf16[128,128]{1,0:T(8,128)(2,1)}, u32[]{:S(2)}) copy-start(bf16[128,128]{1,0:T(8,128)(2,1)} %param.19) | copy-start | bytes 98308
Sparse Core Ops, SparseCore 0:
  27.1 19.4 reduce-scatter.2
  67.8 31.8 reduce-scatter.4
where the time goes:
time: 109 us
  waiting for transfers between devices  50.7 us (47%)
  blocking collectives  24.2 us (22%)
  between operations  14.5 us (13%)
  other arithmetic  6.89 us (6%)
  matrix products  6.53 us (6%)
  local copies, waits for them, and re-layouts  5.81 us (5%)
    reduce_scatter x1, waiting for transfers between devices, per_device(): lax.psum_scatter(jnp.einsum('ijh,ikh->jkh', tri_rows, a_bf, preferred_ele...  31.1 us
    reduce_scatter x1, waiting for transfers between devices, per_device(): lax.psum_scatter(jnp.einsum('jkh,ikh->jih', b_every, a_bf, preferred_elem...  19.6 us
    all_gather x1, blocking collectives, per_device(): tri_rows = lax.all_gather(d_tri, 'col', axis=1, tiled=True)  13.4 us
    all_gather x1, blocking collectives, per_device(): b_every = lax.all_gather(b_bf, 'row', axis=0, tiled=True)  10.8 us
    all_gather x1, local copies, waits for them, and re-layouts, per_device(): b_every = lax.all_gather(b_bf, 'row', axis=0, tiled=True)  2.95 us
  transfers between devices with their start and end apart: 2, of which 2 were waited for; matrix products, arithmetic and copies ran while one was open for 1% of the time, Pallas kernels for 0%

commit v1 on v0

v1 whole, which is shorter than its diff:
```python
import functools

import jax
import jax.numpy as jnp
from jax import lax
from jax.experimental import pallas as pl
from jax.experimental.pallas import tpu as pltpu
from jax.sharding import PartitionSpec as P

F32 = jnp.float32
BF16 = jnp.bfloat16
MESH = pl.DeviceIdType.MESH


def flip(index, step, size):
    if size & (size - 1):
        return lax.rem(index + step, size)
    partner, weight = 0, 1
    while weight < size:
        mine, other = (index // weight) % 2, (step // weight) % 2
        partner = partner + weight * ((mine + other) % 2)
        weight *= 2
    return partner


def source(index, step, size):
    if size & (size - 1):
        return lax.rem(index + size - step, size)
    return flip(index, step, size)


def normalize(values):
    centred = values - jnp.mean(values, -1, keepdims=True)
    inv_std = lax.rsqrt(jnp.mean(centred * centred, -1, keepdims=True) + 1e-05)
    return centred * inv_std, inv_std


def norm_back(upstream, hat, inv_std, gain):
    scaled = upstream * gain
    return inv_std * (
        scaled
        - jnp.mean(scaled, -1, keepdims=True)
        - hat * jnp.mean(scaled * hat, -1, keepdims=True)
    )


def dot(lhs, rhs):
    return jnp.dot(lhs, rhs, preferred_element_type=F32)


def dot_t(lhs, rhs):
    return lax.dot_general(lhs, rhs, (((1,), (1,)), ((), ())), preferred_element_type=F32)


def kernel(
    n_row, n_col, ti, tj,
    pair_ref, mask_ref, gin_ref, bin_ref, wp_ref, bp_ref, wg_ref, bg_ref,
    gmid_ref, bmid_ref, wo_ref, bo_ref, cot_ref,
    upd_ref, grad_ref,
    stage, a_f, b_out, b_in, b_f, tri_own, tri_out, tri_in, d_out_s, d_in, d_f, gb_own, gb_out, gb_in,
    b_ss, b_rs, t_ss, t_rs, d_ss, d_rs, g_ss, g_rs,
):
    row, col = lax.axis_index("row"), lax.axis_index("col")
    tok = ti * tj
    half = ti * ti
    per = tj // ti
    hid = a_f.shape[-1]

    barrier = pltpu.get_barrier_semaphore()
    for step in range(1, n_row):
        pl.semaphore_signal(barrier, inc=1, device_id=(flip(row, step, n_row), col), device_id_type=MESH)
    for step in range(1, n_col):
        pl.semaphore_signal(barrier, inc=1, device_id=(row, flip(col, step, n_col)), device_id_type=MESH)

    def reorder(ref):
        stage[...] = ref[...].astype(F32).reshape(tok, hid)
        return jnp.concatenate([stage[pl.ds(k, ti, stride=tj), :] for k in range(tj)], 0)

    hat_in, rstd_in = normalize(reorder(pair_ref))
    x_bf = (hat_in * gin_ref[...] + bin_ref[...]).astype(BF16)
    proj = dot(x_bf, wp_ref[...]) + bp_ref[...]
    mask_v = mask_ref[...].astype(F32)
    mask = jnp.concatenate(
        [jnp.broadcast_to(mask_v[:, k : k + 1], (ti, hid)) for k in range(tj)], 0
    )
    sig_b = jax.nn.sigmoid(proj[:, 2 * hid : 3 * hid])
    val_b = proj[:, 3 * hid :]
    b_bf = (mask * sig_b * val_b).astype(BF16)
    b_out[...] = b_bf

    pl.semaphore_wait(barrier, n_row + n_col - 2)

    def send_b(step):
        to = flip(row, step, n_row)
        return pltpu.make_async_remote_copy(
            b_out, b_in.at[row], b_ss.at[step], b_rs.at[step],
            device_id=(to, col), device_id_type=MESH,
        )

    for step in range(n_row - 1, 0, -1):
        send_b(step).start()

    sig_a = jax.nn.sigmoid(proj[:, :hid])
    val_a = proj[:, hid : 2 * hid]
    a_f[...] = (mask * sig_a * val_a).astype(BF16).astype(F32)
    b_f[row] = b_bf.astype(F32)

    def send_tri(block):
        to = block // per
        part = block % per
        return pltpu.make_async_remote_copy(
            tri_out.at[block], tri_in.at[col, part], t_ss.at[block], t_rs.at[col, part],
            device_id=(row, to), device_id_type=MESH,
        )

    def forward(block):
        sums = []
        a_k = [a_f[k * ti : (k + 1) * ti, :] for k in range(tj)]
        for jj in range(ti):
            total = None
            for k in range(tj):
                term = a_k[k] * b_f[block, k * ti + jj : k * ti + jj + 1, :]
                total = term if total is None else total + term
            sums.append(total)
        whole = jnp.concatenate(sums, 0)

        @pl.when(block // per == col)
        def _():
            tri_own[block % per] = whole

        @pl.when(block // per != col)
        def _():
            tri_out[block] = whole.astype(BF16)
            send_tri(block).start()

    forward(row)

    def forward_step(step, carry):
        block = source(row, step, n_row)
        pltpu.make_async_remote_copy(
            b_out, b_in.at[block], b_ss.at[step], b_rs.at[step],
            device_id=(block, col), device_id_type=MESH,
        ).wait_recv()
        b_f[block] = b_in[block].astype(F32)
        forward(block)
        return carry

    lax.fori_loop(1, n_row, forward_step, 0)

    gate = jax.nn.sigmoid(dot(x_bf, wg_ref[...]) + bg_ref[...])
    grad_out = reorder(cot_ref)
    d_out = (grad_out * gate).astype(BF16)
    d_mid = dot_t(d_out, wo_ref[...])

    triangle = jnp.concatenate([tri_own[part] for part in range(per)], 0)
    for step in range(1, n_col):
        other = source(col, step, n_col)
        for part in range(per):
            pltpu.make_async_remote_copy(
                tri_out.at[0], tri_in.at[other, part], t_ss.at[0], t_rs.at[other, part],
                device_id=(row, other), device_id_type=MESH,
            ).wait_recv()
        triangle = triangle + jnp.concatenate(
            [tri_in[other, part].astype(F32) for part in range(per)], 0
        )
    hat_mid, rstd_mid = normalize(triangle)
    d_tri = norm_back(d_mid, hat_mid, rstd_mid, gmid_ref[...]).astype(BF16)
    d_out_s[...] = d_tri

    def send_d(step):
        to = flip(col, step, n_col)
        return pltpu.make_async_remote_copy(
            d_out_s, d_in.at[col], d_ss.at[step], d_rs.at[step],
            device_id=(row, to), device_id_type=MESH,
        )

    for step in range(n_col - 1, 0, -1):
        send_d(step).start()
    d_f[pl.ds(col * tok, tok), :] = d_tri.astype(F32)

    def send_gb(block):
        return pltpu.make_async_remote_copy(
            gb_out.at[block], gb_in.at[row], g_ss.at[block], g_rs.at[row],
            device_id=(block, col), device_id_type=MESH,
        )

    def backward_b(block):
        d_i = [d_f[pl.ds(block * half + i, ti, stride=ti), :] for i in range(ti)]
        sums = []
        for k in range(tj):
            total = None
            for i in range(ti):
                term = d_i[i] * a_f[k * ti + i : k * ti + i + 1, :]
                total = term if total is None else total + term
            sums.append(total)
        whole = jnp.concatenate(sums, 0)

        @pl.when(block == row)
        def _():
            gb_own[...] = whole

        @pl.when(block != row)
        def _():
            gb_out[block] = whole.astype(BF16)
            send_gb(block).start()

    for part in range(per):
        backward_b(col * per + part)

    mid_bf = (hat_mid * gmid_ref[...] + bmid_ref[...]).astype(BF16)
    out_lin = dot(mid_bf, wo_ref[...]) + bo_ref[...]
    update = gate * out_lin
    for k in range(tj):
        stage[pl.ds(k, ti, stride=tj), :] = update[k * ti : (k + 1) * ti, :]
    upd_ref[...] = stage[...].astype(BF16).reshape(ti, tj, hid)
    d_gpre = (grad_out * out_lin * gate * (1.0 - gate)).astype(BF16)

    def backward_step(step, carry):
        other = source(col, step, n_col)
        pltpu.make_async_remote_copy(
            d_out_s, d_in.at[other], d_ss.at[step], d_rs.at[step],
            device_id=(row, other), device_id_type=MESH,
        ).wait_recv()
        d_f[pl.ds(other * tok, tok), :] = d_in[other].astype(F32)
        for part in range(per):
            backward_b(other * per + part)
        return carry

    lax.fori_loop(1, n_col, backward_step, 0)

    def backward_a(block, sums):
        out = list(sums)
        for jj in range(ti):
            d_j = d_f[pl.ds(block * half + jj * ti, ti), :]
            for k in range(tj):
                out[k] = out[k] + d_j * b_f[block, k * ti + jj : k * ti + jj + 1, :]
        return tuple(out)

    zero = tuple(jnp.zeros((ti, hid), F32) for _ in range(tj))
    grad_a = jnp.concatenate(lax.fori_loop(0, n_row, backward_a, zero), 0) * mask
    d_ga = (grad_a * val_a * sig_a * (1.0 - sig_a)).astype(BF16)
    d_va = (grad_a * sig_a).astype(BF16)
    d_x = (
        dot_t(d_gpre, wg_ref[...])
        + dot_t(d_ga, wp_ref[:, :hid])
        + dot_t(d_va, wp_ref[:, hid : 2 * hid])
    )

    grad_b = gb_own[...]
    for step in range(1, n_row):
        other = source(row, step, n_row)
        pltpu.make_async_remote_copy(
            gb_out.at[0], gb_in.at[other], g_ss.at[0], g_rs.at[other],
            device_id=(other, col), device_id_type=MESH,
        ).wait_recv()
        grad_b = grad_b + gb_in[other].astype(F32)
    grad_b = grad_b * mask
    d_gb = (grad_b * val_b * sig_b * (1.0 - sig_b)).astype(BF16)
    d_vb = (grad_b * sig_b).astype(BF16)
    d_x = d_x + dot_t(d_gb, wp_ref[:, 2 * hid : 3 * hid]) + dot_t(d_vb, wp_ref[:, 3 * hid :])
    pair_grad = norm_back(d_x, hat_in, rstd_in, gin_ref[...])
    for k in range(tj):
        stage[pl.ds(k, ti, stride=tj), :] = pair_grad[k * ti : (k + 1) * ti, :]
    grad_ref[...] = stage[...].reshape(ti, tj, hid)

    for step in range(1, n_row):
        send_b(step).wait_send()
    for block in range(n_row):
        @pl.when(block // per != col)
        def _():
            send_tri(block).wait_send()
    for step in range(1, n_col):
        send_d(step).wait_send()
    for block in range(n_row):
        @pl.when(block != row)
        def _():
            send_gb(block).wait_send()


def per_device(n_row, n_col, pair, pair_mask, gin, bin_, wp, bp, wg, bg, gmid, bmid, wo, bo, cot):
    ti, tj, chan = pair.shape
    hid = chan
    tok, per = ti * tj, tj // ti
    vec = lambda v: v.reshape(1, -1)
    dma = pltpu.SemaphoreType.DMA
    vmem = pl.BlockSpec(memory_space=pltpu.VMEM)
    return pl.pallas_call(
        functools.partial(kernel, n_row, n_col, ti, tj),
        name="triangle_step",
        out_shape=(
            jax.ShapeDtypeStruct(pair.shape, BF16),
            jax.ShapeDtypeStruct(pair.shape, F32),
        ),
        in_specs=[vmem] * 13,
        out_specs=(vmem, vmem),
        scratch_shapes=[
            pltpu.VMEM((tok, hid), F32),
            pltpu.VMEM((tok, hid), F32),
            pltpu.VMEM((tok, hid), BF16),
            pltpu.VMEM((n_row, tok, hid), BF16),
            pltpu.VMEM((n_row, tok, hid), F32),
            pltpu.VMEM((per, ti * ti, hid), F32),
            pltpu.VMEM((n_row, ti * ti, hid), BF16),
            pltpu.VMEM((n_col, per, ti * ti, hid), BF16),
            pltpu.VMEM((tok, hid), BF16),
            pltpu.VMEM((n_col, tok, hid), BF16),
            pltpu.VMEM((n_col * tok, hid), F32),
            pltpu.VMEM((tok, hid), F32),
            pltpu.VMEM((n_row, tok, hid), BF16),
            pltpu.VMEM((n_row, tok, hid), BF16),
            dma((n_row,)),
            dma((n_row,)),
            dma((n_row,)),
            dma((n_col, per)),
            dma((n_col,)),
            dma((n_col,)),
            dma((n_row,)),
            dma((n_row,)),
        ],
        compiler_params=pltpu.CompilerParams(
            collective_id=0, has_side_effects=True, vmem_limit_bytes=40 << 20
        ),
    )(pair, pair_mask, vec(gin), vec(bin_), wp, vec(bp), wg, vec(bg), vec(gmid), vec(bmid), wo, vec(bo), cot)


def solution(mesh):
    grid = P("row", "col", None)
    placed = (grid, P("row", "col")) + (P(),) * 10 + (grid,)
    return jax.shard_map(
        functools.partial(per_device, mesh.shape["row"], mesh.shape["col"]),
        mesh=mesh,
        in_specs=placed,
        out_specs=(grid, grid),
        check_vma=False,
    )
```

time: 109 us -> 29.8 us (0.27)
  waiting for transfers between devices: 50.7 us -> 0 us
  blocking collectives: 24.2 us -> 0 us
  Pallas kernels: 0 us -> 22.8 us
  between operations: 14.5 us -> 0.72 us
  other arithmetic: 6.89 us -> 0 us
  matrix products: 6.53 us -> 0 us
    reduce_scatter x2 -> x0, waiting for transfers between devices: 50.7 us -> none  [the longest x1 31.1 us: per_device(): lax.psum_scatter(jnp.einsum('ijh,ikh->jkh', tri_rows, a_bf, preferred_ele...]
    all_gather x2 -> x0, blocking collectives: 24.2 us -> none  [the longest x1 13.4 us: per_device(): tri_rows = lax.all_gather(d_tri, 'col', axis=1, tiled=True)]
    pallas_call x0 -> x1, Pallas kernels: none -> 22.8 us  [per_device(): pl.pallas_call(functools.partial(kernel, n_row, n_col, ti, tj), name='tri...]
    dot_general x9 -> x0, matrix products: 6.53 us -> none  [the longest x1 1.18 us: per_device(): jnp.einsum('jkh,ikh->jih', b_every, a_bf, preferred_element_type=jnp.floa...]
    unnamed x36 -> x28, local copies, waits for them, and re-layouts: 0.11 us -> 5.88 us
    reduce_sum x4 -> x0, other arithmetic: 3.53 us -> none  [the longest x2 1.84 us: layer_norm(): inv_std = lax.rsqrt(jnp.mean(centred * centred, -1, keepdims=True) + 1e-05)]
    all_gather x2 -> x0, local copies, waits for them, and re-layouts: 3.17 us -> none  [the longest x1 2.95 us: per_device(): b_every = lax.all_gather(b_bf, 'row', axis=0, tiled=True)]
    convert_element_type x3 -> x0, other arithmetic: 1.7 us -> none  [the longest x1 0.89 us: per_device(): norm_back(d_mid, hat_mid, rstd_mid, ln_mid_gain).astype(jnp.bfloat16)]
  transfers between devices with their start and end apart: 2 -> 0, of which waited for: 2 -> 0; matrix products, arithmetic and copies ran while one was open for 1% -> 0% of each run, Pallas kernels for 0% -> 0%
where the time goes in v1:
time: 29.8 us; the launch traced here: 29.4 us
  Pallas kernels  22.8 us (77%)
  local copies, waits for them, and re-layouts  5.88 us (20%)
  between operations  0.72 us (2%)
    pallas_call x1, Pallas kernels, per_device(): pl.pallas_call(functools.partial(kernel, n_row, n_col, ti, tj), name='tri...  22.8 us
    unnamed x28, local copies, waits for them, and re-layouts  5.88 us

profile of v1, /device:TPU:0, one launch (start us, length us, event | category | flops | bytes accessed | tf_op | source)
XLA Modules:
  0.0 29.4 jit_solution(6166911488011562723)
XLA Ops:
  0.6 0.0 copy-start.10
  0.6 0.0 copy-start.11
  0.7 0.0 copy-start.12
  0.7 0.0 copy-start.5
  0.7 0.0 copy-start.6
  0.7 0.0 copy-start.7
  0.7 0.0 copy-start.8
  0.7 0.0 copy-start.9
  0.7 0.6 %copy-done.10 = f32[128]{0:T(128)S(1)} copy-done((f32[128]{0:T(128)S(1)}, f32[128]{0:T(128)}, u32[]{:S(2)}) %copy-start.10) | copy-done | bytes 536
  1.3 0.0 copy-done.11
  1.3 0.0 copy-done.12
  1.3 0.0 copy-done.5
  1.4 0.0 copy-done.6
  1.4 0.0 copy-done.7
  1.4 0.0 copy-done.8
  1.4 0.0 copy-done.9
  1.4 0.0 copy-start
  1.4 0.9 %copy-done = bf16[128,512]{1,0:T(8,128)(2,1)S(1)} copy-done((bf16[128,512]{1,0:T(8,128)(2,1)S(1)}, bf16[128,512]{1,0:T(8,128)(2,1)}, u32[]{:S(2)}) %copy-start) | copy-done | bytes 131096
  2.3 0.0 copy-start.1
  2.3 0.8 %copy-done.1 = bf16[8,16,128]{2,1,0:T(8,128)(2,1)S(1)} copy-done((bf16[8,16,128]{2,1,0:T(8,128)(2,1)S(1)}, bf16[8,16,128]{2,1,0:T(8,128)(2,1)}, u32[]{:S(2)}) %copy-start.1) | copy-done | bytes 32792
  3.1 0.0 copy-start.2
  3.1 0.8 %copy-done.2 = bf16[128,128]{1,0:T(8,128)(2,1)S(1)} copy-done((bf16[128,128]{1,0:T(8,128)(2,1)S(1)}, bf16[128,128]{1,0:T(8,128)(2,1)}, u32[]{:S(2)}) %copy-start.2) | copy-done | bytes 32792
  3.8 0.0 copy-start.3
  3.8 0.8 %copy-done.3 = bf16[128,128]{1,0:T(8,128)(2,1)S(1)} copy-done((bf16[128,128]{1,0:T(8,128)(2,1)S(1)}, bf16[128,128]{1,0:T(8,128)(2,1)}, u32[]{:S(2)}) %copy-start.3) | copy-done | bytes 32792
  4.6 0.0 copy-start.4
  4.6 0.8 %copy-done.4 = bf16[8,16,128]{2,1,0:T(8,128)(2,1)S(1)} copy-done((bf16[8,16,128]{2,1,0:T(8,128)(2,1)S(1)}, bf16[8,16,128]{2,1,0:T(8,128)(2,1)}, u32[]{:S(2)}) %copy-start.4) | copy-done | bytes 32792
  5.3 22.8 %triangle_step.1 = (bf16[8,16,128]{2,1,0:T(8,128)(2,1)S(1)}, f32[8,16,128]{2,1,0:T(8,128)S(1)}) custom-call(bf16[8,16,128]{2,1,0:T(8,128)(2,1)S(1)} %copy-done.1, s32[8,16]{1,0:T(8,128)S(1)} %copy-done.5, f32[1,128]{1,0:T(1,128)S(1)} %bitcast.8, f32[1,128]{1,0:T(1,128)S(1)} %bitcast.9, bf16[128,512]{1,0:T(8,128)(2,1)S(1)} %copy-done, f32[1,512]{1,0:T(1,128)S(1)} %bitcast.7, ...), custom_call_target="tpu_custom_call" | custom-call | tf_op jit(solution)/shard_map/triangle_step/pallas_call | solution.py:287
  28.1 0.6 %copy.17 = bf16[8,16,128]{2,1,0:T(8,128)(2,1)} copy(bf16[8,16,128]{2,1,0:T(8,128)(2,1)S(1)} %get-tuple-element.4) | data formatting | bytes 65536
  28.8 0.6 %copy.18 = f32[8,16,128]{2,1,0:T(8,128)} copy(f32[8,16,128]{2,1,0:T(8,128)S(1)} %get-tuple-element.5) | data formatting | bytes 131072
Async XLA Ops:
  0.6 0.7 %copy-start.10 = (f32[128]{0:T(128)S(1)}, f32[128]{0:T(128)}, u32[]{:S(2)}) copy-start(f32[128]{0:T(128)} %param.21) | copy-start | bytes 1540
  0.6 0.7 %copy-start.11 = (f32[128]{0:T(128)S(1)}, f32[128]{0:T(128)}, u32[]{:S(2)}) copy-start(f32[128]{0:T(128)} %param.22) | copy-start | bytes 1540
  0.7 0.7 %copy-start.12 = (f32[128]{0:T(128)S(1)}, f32[128]{0:T(128)}, u32[]{:S(2)}) copy-start(f32[128]{0:T(128)} %param.24) | copy-start | bytes 1540
  0.7 0.7 %copy-start.5 = (s32[8,16]{1,0:T(8,128)S(1)}, s32[8,16]{1,0:T(8,128)}, u32[]{:S(2)}) copy-start(s32[8,16]{1,0:T(8,128)} %mask_ref.1) | copy-start | bytes 1540
  0.7 0.7 %copy-start.6 = (f32[512]{0:T(512)S(1)}, f32[512]{0:T(512)}, u32[]{:S(2)}) copy-start(f32[512]{0:T(512)} %param.18) | copy-start | bytes 6148
  0.7 0.7 %copy-start.7 = (f32[128]{0:T(128)S(1)}, f32[128]{0:T(128)}, u32[]{:S(2)}) copy-start(f32[128]{0:T(128)} %param.15) | copy-start | bytes 1540
  0.7 0.7 %copy-start.8 = (f32[128]{0:T(128)S(1)}, f32[128]{0:T(128)}, u32[]{:S(2)}) copy-start(f32[128]{0:T(128)} %param.16) | copy-start | bytes 1540
  0.7 0.7 %copy-start.9 = (f32[128]{0:T(128)S(1)}, f32[128]{0:T(128)}, u32[]{:S(2)}) copy-start(f32[128]{0:T(128)} %param.20) | copy-start | bytes 1540
  1.4 0.9 %copy-start = (bf16[128,512]{1,0:T(8,128)(2,1)S(1)}, bf16[128,512]{1,0:T(8,128)(2,1)}, u32[]{:S(2)}) copy-start(bf16[128,512]{1,0:T(8,128)(2,1)} %wp_ref.1) | copy-start | bytes 393220
  2.3 0.8 %copy-start.1 = (bf16[8,16,128]{2,1,0:T(8,128)(2,1)S(1)}, bf16[8,16,128]{2,1,0:T(8,128)(2,1)}, u32[]{:S(2)}) copy-start(bf16[8,16,128]{2,1,0:T(8,128)(2,1)} %pair_ref.1) | copy-start | bytes 98308
  3.1 0.8 %copy-start.2 = (bf16[128,128]{1,0:T(8,128)(2,1)S(1)}, bf16[128,128]{1,0:T(8,128)(2,1)}, u32[]{:S(2)}) copy-start(bf16[128,128]{1,0:T(8,128)(2,1)} %wg_ref.1) | copy-start | bytes 98308
  3.8 0.8 %copy-start.3 = (bf16[128,128]{1,0:T(8,128)(2,1)S(1)}, bf16[128,128]{1,0:T(8,128)(2,1)}, u32[]{:S(2)}) copy-start(bf16[128,128]{1,0:T(8,128)(2,1)} %wo_ref.1) | copy-start | bytes 98308
  4.6 0.8 %copy-start.4 = (bf16[8,16,128]{2,1,0:T(8,128)(2,1)S(1)}, bf16[8,16,128]{2,1,0:T(8,128)(2,1)}, u32[]{:S(2)}) copy-start(bf16[8,16,128]{2,1,0:T(8,128)(2,1)} %cot_ref.1) | copy-start | bytes 98308

commit v2 on v1

--- a/solution.py
+++ b/solution.py
@@ -54,9 +54,11 @@
 
 def kernel(
     n_row, n_col, ti, tj,
+    pair_hbm, mask_hbm, gin_hbm, bin_hbm, wp_hbm, bp_hbm, wg_hbm, bg_hbm,
+    gmid_hbm, bmid_hbm, wo_hbm, bo_hbm, cot_hbm,
+    upd_ref, grad_ref,
     pair_ref, mask_ref, gin_ref, bin_ref, wp_ref, bp_ref, wg_ref, bg_ref,
-    gmid_ref, bmid_ref, wo_ref, bo_ref, cot_ref,
-    upd_ref, grad_ref,
+    gmid_ref, bmid_ref, wo_ref, bo_ref, cot_ref, in_sem,
     stage, a_f, b_out, b_in, b_f, tri_own, tri_out, tri_in, d_out_s, d_in, d_f, gb_own, gb_out, gb_in,
     b_ss, b_rs, t_ss, t_rs, d_ss, d_rs, g_ss, g_rs,
 ):
@@ -66,6 +68,18 @@
     per = tj // ti
     hid = a_f.shape[-1]
 
+    operands = (
+        (pair_hbm, pair_ref), (wp_hbm, wp_ref), (gin_hbm, gin_ref), (bin_hbm, bin_ref),
+        (bp_hbm, bp_ref), (mask_hbm, mask_ref), (wg_hbm, wg_ref), (bg_hbm, bg_ref),
+        (cot_hbm, cot_ref), (wo_hbm, wo_ref), (gmid_hbm, gmid_ref), (bmid_hbm, bmid_ref),
+        (bo_hbm, bo_ref),
+    )
+    loads = [
+        pltpu.make_async_copy(src, dst, in_sem.at[n]) for n, (src, dst) in enumerate(operands)
+    ]
+    for load in loads:
+        load.start()
+
     barrier = pltpu.get_barrier_semaphore()
     for step in range(1, n_row):
         pl.semaphore_signal(barrier, inc=1, device_id=(flip(row, step, n_row), col), device_id_type=MESH)
@@ -76,7 +90,10 @@
         stage[...] = ref[...].astype(F32).reshape(tok, hid)
         return jnp.concatenate([stage[pl.ds(k, ti, stride=tj), :] for k in range(tj)], 0)
 
+    loads[0].wait()
     hat_in, rstd_in = normalize(reorder(pair_ref))
+    for load in loads[1:6]:
+        load.wait()
     x_bf = (hat_in * gin_ref[...] + bin_ref[...]).astype(BF16)
     proj = dot(x_bf, wp_ref[...]) + bp_ref[...]
     mask_v = mask_ref[...].astype(F32)
@@ -147,6 +164,8 @@
 
     lax.fori_loop(1, n_row, forward_step, 0)
 
+    for load in loads[6:]:
+        load.wait()
     gate = jax.nn.sigmoid(dot(x_bf, wg_ref[...]) + bg_ref[...])
     grad_out = reorder(cot_ref)
     d_out = (grad_out * gate).astype(BF16)
@@ -284,6 +303,7 @@
     vec = lambda v: v.reshape(1, -1)
     dma = pltpu.SemaphoreType.DMA
     vmem = pl.BlockSpec(memory_space=pltpu.VMEM)
+    operands = (pair, pair_mask, vec(gin), vec(bin_), wp, vec(bp), wg, vec(bg), vec(gmid), vec(bmid), wo, vec(bo), cot)
     return pl.pallas_call(
         functools.partial(kernel, n_row, n_col, ti, tj),
         name="triangle_step",
@@ -291,9 +311,11 @@
             jax.ShapeDtypeStruct(pair.shape, BF16),
             jax.ShapeDtypeStruct(pair.shape, F32),
         ),
-        in_specs=[vmem] * 13,
+        in_specs=[pl.BlockSpec(memory_space=pltpu.HBM)] * 13,
         out_specs=(vmem, vmem),
-        scratch_shapes=[
+        scratch_shapes=[pltpu.VMEM(v.shape, v.dtype) for v in operands]
+        + [dma((len(operands),))]
+        + [
             pltpu.VMEM((tok, hid), F32),
             pltpu.VMEM((tok, hid), F32),
             pltpu.VMEM((tok, hid), BF16),
@@ -318,9 +340,9 @@
             dma((n_row,)),
         ],
         compiler_params=pltpu.CompilerParams(
-            collective_id=0, has_side_effects=True, vmem_limit_bytes=40 << 20
+            collective_id=0, has_side_effects=True, vmem_limit_bytes=56 << 20
         ),
-    )(pair, pair_mask, vec(gin), vec(bin_), wp, vec(bp), wg, vec(bg), vec(gmid), vec(bmid), wo, vec(bo), cot)
+    )(*operands)
 
 
 def solution(mesh):

time: 29.8 us -> 26.6 us (0.89)
  local copies, waits for them, and re-layouts: 5.88 us -> 2.04 us
  Pallas kernels: 22.8 us -> 23.7 us
    unnamed x28 -> x4, local copies, waits for them, and re-layouts: 5.88 us -> 2.04 us
    pallas_call x1, Pallas kernels: 22.8 us -> 23.7 us  [per_device(): pl.pallas_call(functools.partial(kernel, n_row, n_col, ti, tj), name='tri...]
where the time goes in v2:
time: 26.6 us; the launch traced here: 26.4 us
  Pallas kernels  23.7 us (89%)
  local copies, waits for them, and re-layouts  2.04 us (8%)
  between operations  0.65 us (2%)
    pallas_call x1, Pallas kernels, per_device(): pl.pallas_call(functools.partial(kernel, n_row, n_col, ti, tj), name='tri...  23.7 us
    unnamed x4, local copies, waits for them, and re-layouts  2.04 us

profile of v2, /device:TPU:0, one launch (start us, length us, event | category | flops | bytes accessed | tf_op | source)
XLA Modules:
  0.0 26.4 jit_solution(8341211881051916303)
XLA Ops:
  0.6 23.7 %triangle_step.1 = (bf16[8,16,128]{2,1,0:T(8,128)(2,1)}, f32[8,16,128]{2,1,0:T(8,128)}) custom-call(bf16[8,16,128]{2,1,0:T(8,128)(2,1)} %pair_hbm.1, s32[8,16]{1,0:T(8,128)} %mask_hbm.1, f32[1,128]{1,0:T(1,128)} %bitcast.8, f32[1,128]{1,0:T(1,128)} %bitcast.9, bf16[128,512]{1,0:T(8,128)(2,1)} %wp_hbm.1, f32[1,512]{1,0:T(1,128)} %bitcast.7, ...), custom_call_target="tpu_custom_call" | custom-call | tf_op jit(solution)/shard_map/triangle_step/pallas_call | solution.py:307
  24.3 0.0 copy-start
  24.4 1.4 %copy.17 = bf16[8,16,128]{2,1,0:T(8,128)(2,1)} copy(bf16[8,16,128]{2,1,0:T(8,128)(2,1)} %get-tuple-element.4) | data formatting | bytes 65536
  25.8 0.0 copy-done
  25.8 0.6 %copy.18 = f32[8,16,128]{2,1,0:T(8,128)} copy(f32[8,16,128]{2,1,0:T(8,128)S(1)} %copy-done) | data formatting | bytes 131072
Async XLA Ops:
  24.3 1.4 %copy-start = (f32[8,16,128]{2,1,0:T(8,128)S(1)}, f32[8,16,128]{2,1,0:T(8,128)}, u32[]{:S(2)}) copy-start(f32[8,16,128]{2,1,0:T(8,128)} %get-tuple-element.5) | copy-start | bytes 196612

commit v3 on v2

--- a/solution.py
+++ b/solution.py
@@ -95,13 +95,13 @@
     for load in loads[1:6]:
         load.wait()
     x_bf = (hat_in * gin_ref[...] + bin_ref[...]).astype(BF16)
-    proj = dot(x_bf, wp_ref[...]) + bp_ref[...]
+    proj_b = dot(x_bf, wp_ref[:, 2 * hid :]) + bp_ref[:, 2 * hid :]
     mask_v = mask_ref[...].astype(F32)
     mask = jnp.concatenate(
         [jnp.broadcast_to(mask_v[:, k : k + 1], (ti, hid)) for k in range(tj)], 0
     )
-    sig_b = jax.nn.sigmoid(proj[:, 2 * hid : 3 * hid])
-    val_b = proj[:, 3 * hid :]
+    sig_b = jax.nn.sigmoid(proj_b[:, :hid])
+    val_b = proj_b[:, hid:]
     b_bf = (mask * sig_b * val_b).astype(BF16)
     b_out[...] = b_bf
 
@@ -117,8 +117,9 @@
     for step in range(n_row - 1, 0, -1):
         send_b(step).start()
 
-    sig_a = jax.nn.sigmoid(proj[:, :hid])
-    val_a = proj[:, hid : 2 * hid]
+    proj_a = dot(x_bf, wp_ref[:, : 2 * hid]) + bp_ref[:, : 2 * hid]
+    sig_a = jax.nn.sigmoid(proj_a[:, :hid])
+    val_a = proj_a[:, hid:]
     a_f[...] = (mask * sig_a * val_a).astype(BF16).astype(F32)
     b_f[row] = b_bf.astype(F32)
 
@@ -296,6 +297,15 @@
             send_gb(block).wait_send()
 
 
+def store(upd_ref, grad_ref, upd_hbm, grad_hbm, sem):
+    first = pltpu.make_async_copy(upd_ref, upd_hbm, sem.at[0])
+    second = pltpu.make_async_copy(grad_ref, grad_hbm, sem.at[1])
+    second.start()
+    first.start()
+    second.wait()
+    first.wait()
+
+
 def per_device(n_row, n_col, pair, pair_mask, gin, bin_, wp, bp, wg, bg, gmid, bmid, wo, bo, cot):
     ti, tj, chan = pair.shape
     hid = chan
@@ -304,7 +314,7 @@
     dma = pltpu.SemaphoreType.DMA
     vmem = pl.BlockSpec(memory_space=pltpu.VMEM)
     operands = (pair, pair_mask, vec(gin), vec(bin_), wp, vec(bp), wg, vec(bg), vec(gmid), vec(bmid), wo, vec(bo), cot)
-    return pl.pallas_call(
+    update, grad = pl.pallas_call(
         functools.partial(kernel, n_row, n_col, ti, tj),
         name="triangle_step",
         out_shape=(
@@ -340,9 +350,22 @@
             dma((n_row,)),
         ],
         compiler_params=pltpu.CompilerParams(
-            collective_id=0, has_side_effects=True, vmem_limit_bytes=56 << 20
+            collective_id=0, has_side_effects=True, vmem_limit_bytes=40 << 20
         ),
-    )(*operands)
+    )(*[pltpu.with_memory_space_constraint(v, pltpu.HBM) for v in operands])
+    hbm = pl.BlockSpec(memory_space=pltpu.HBM)
+    return pl.pallas_call(
+        store,
+        name="store_outputs",
+        out_shape=(
+            jax.ShapeDtypeStruct(pair.shape, BF16),
+            jax.ShapeDtypeStruct(pair.shape, F32),
+        ),
+        in_specs=[vmem, vmem],
+        out_specs=(hbm, hbm),
+        scratch_shapes=[dma((2,))],
+        compiler_params=pltpu.CompilerParams(vmem_limit_bytes=1 << 20),
+    )(update, grad)
 
 
 def solution(mesh):

time: 26.6 us -> 24.5 us (0.921)
  local copies, waits for them, and re-layouts: 2.04 us -> 0 us
    unnamed x4 -> x0, local copies, waits for them, and re-layouts: 2.04 us -> none
    pallas_call x0 -> x1, Pallas kernels: none -> 0.66 us  [per_device(): pl.pallas_call(store, name='store_outputs', out_shape=(jax.ShapeDtypeStru...]
    pallas_call x1, Pallas kernels: 23.7 us -> 23.1 us  [per_device(): pl.pallas_call(functools.partial(kernel, n_row, n_col, ti, tj), name='tri...]
where the time goes in v3:
time: 24.5 us; the launch traced here: 24.4 us
  Pallas kernels  23.7 us (97%)
  between operations  0.64 us (3%)
    pallas_call x1, Pallas kernels, per_device(): pl.pallas_call(functools.partial(kernel, n_row, n_col, ti, tj), name='tri...  23.1 us
    pallas_call x1, Pallas kernels, per_device(): pl.pallas_call(store, name='store_outputs', out_shape=(jax.ShapeDtypeStru...  0.66 us

profile of v3, /device:TPU:0, one launch (start us, length us, event | category | flops | bytes accessed | tf_op | source)
XLA Modules:
  0.0 24.4 jit_solution(6690587098317851730)
XLA Ops:
  0.6 23.1 %triangle_step.1 = (bf16[8,16,128]{2,1,0:T(8,128)(2,1)S(1)}, f32[8,16,128]{2,1,0:T(8,128)S(1)}) custom-call(bf16[8,16,128]{2,1,0:T(8,128)(2,1)} %pair_hbm.1, s32[8,16]{1,0:T(8,128)} %mask_hbm.1, f32[1,128]{1,0:T(1,128)} %bitcast.8, f32[1,128]{1,0:T(1,128)} %bitcast.9, bf16[128,512]{1,0:T(8,128)(2,1)} %wp_hbm.1, f32[1,512]{1,0:T(1,128)} %bitcast.7, ...), custom_call_target="tpu_custom_call" | custom-call | tf_op jit(solution)/shard_map/triangle_step/pallas_call | solution.py:317
  23.7 0.7 %store_outputs.1 = (bf16[8,16,128]{2,1,0:T(8,128)(2,1)}, f32[8,16,128]{2,1,0:T(8,128)}) custom-call(bf16[8,16,128]{2,1,0:T(8,128)(2,1)S(1)} %get-tuple-element.4.upd_ref, f32[8,16,128]{2,1,0:T(8,128)S(1)} %get-tuple-element.5.grad_ref), custom_call_target="tpu_custom_call" | custom-call | tf_op jit(solution)/shard_map/store_outputs/pallas_call | solution.py:357

commit v4 on v3

--- a/solution.py
+++ b/solution.py
@@ -114,7 +114,7 @@
             device_id=(to, col), device_id_type=MESH,
         )
 
-    for step in range(n_row - 1, 0, -1):
+    for step in range(1, n_row):
         send_b(step).start()
 
     proj_a = dot(x_bf, wp_ref[:, : 2 * hid]) + bp_ref[:, : 2 * hid]

time: 24.5 us -> 23.8 us (0.971)
  Pallas kernels: 23.7 us -> 23 us
    pallas_call x1, Pallas kernels: 23.1 us -> 22.3 us  [per_device(): pl.pallas_call(functools.partial(kernel, n_row, n_col, ti, tj), name='tri...]
where the time goes in v4:
time: 23.8 us; the launch traced here: 23.6 us
  Pallas kernels  23 us (97%)
  between operations  0.64 us (3%)
    pallas_call x1, Pallas kernels, per_device(): pl.pallas_call(functools.partial(kernel, n_row, n_col, ti, tj), name='tri...  22.3 us
    pallas_call x1, Pallas kernels, per_device(): pl.pallas_call(store, name='store_outputs', out_shape=(jax.ShapeDtypeStru...  0.66 us

profile of v4, /device:TPU:0, one launch (start us, length us, event | category | flops | bytes accessed | tf_op | source)
XLA Modules:
  0.0 23.6 jit_solution(18260695715187725620)
XLA Ops:
  0.6 22.3 %triangle_step.1 = (bf16[8,16,128]{2,1,0:T(8,128)(2,1)S(1)}, f32[8,16,128]{2,1,0:T(8,128)S(1)}) custom-call(bf16[8,16,128]{2,1,0:T(8,128)(2,1)} %pair_hbm.1, s32[8,16]{1,0:T(8,128)} %mask_hbm.1, f32[1,128]{1,0:T(1,128)} %bitcast.8, f32[1,128]{1,0:T(1,128)} %bitcast.9, bf16[128,512]{1,0:T(8,128)(2,1)} %wp_hbm.1, f32[1,512]{1,0:T(1,128)} %bitcast.7, ...), custom_call_target="tpu_custom_call" | custom-call | tf_op jit(solution)/shard_map/triangle_step/pallas_call | solution.py:317
  23.0 0.7 %store_outputs.1 = (bf16[8,16,128]{2,1,0:T(8,128)(2,1)}, f32[8,16,128]{2,1,0:T(8,128)}) custom-call(bf16[8,16,128]{2,1,0:T(8,128)(2,1)S(1)} %get-tuple-element.4.upd_ref, f32[8,16,128]{2,1,0:T(8,128)S(1)} %get-tuple-element.5.grad_ref), custom_call_target="tpu_custom_call" | custom-call | tf_op jit(solution)/shard_map/store_outputs/pallas_call | solution.py:357

commit v5 on v4

--- a/solution.py
+++ b/solution.py
@@ -194,7 +194,7 @@
             device_id=(row, to), device_id_type=MESH,
         )
 
-    for step in range(n_col - 1, 0, -1):
+    for step in range(1, n_col):
         send_d(step).start()
     d_f[pl.ds(col * tok, tok), :] = d_tri.astype(F32)
 

time: 23.8 us -> 23.6 us (level)
  no operation moved by 1% of the time
where the time goes in v5:
time: 23.6 us; the launch traced here: 23.4 us
  Pallas kernels  22.8 us (97%)
  between operations  0.64 us (3%)
    pallas_call x1, Pallas kernels, per_device(): pl.pallas_call(functools.partial(kernel, n_row, n_col, ti, tj), name='tri...  22.1 us
    pallas_call x1, Pallas kernels, per_device(): pl.pallas_call(store, name='store_outputs', out_shape=(jax.ShapeDtypeStru...  0.66 us

profile of v5, /device:TPU:0, one launch (start us, length us, event | category | flops | bytes accessed | tf_op | source)
XLA Modules:
  0.0 23.4 jit_solution(14344107080336498555)
XLA Ops:
  0.6 22.1 %triangle_step.1 = (bf16[8,16,128]{2,1,0:T(8,128)(2,1)S(1)}, f32[8,16,128]{2,1,0:T(8,128)S(1)}) custom-call(bf16[8,16,128]{2,1,0:T(8,128)(2,1)} %pair_hbm.1, s32[8,16]{1,0:T(8,128)} %mask_hbm.1, f32[1,128]{1,0:T(1,128)} %bitcast.8, f32[1,128]{1,0:T(1,128)} %bitcast.9, bf16[128,512]{1,0:T(8,128)(2,1)} %wp_hbm.1, f32[1,512]{1,0:T(1,128)} %bitcast.7, ...), custom_call_target="tpu_custom_call" | custom-call | tf_op jit(solution)/shard_map/triangle_step/pallas_call | solution.py:317
  22.8 0.7 %store_outputs.1 = (bf16[8,16,128]{2,1,0:T(8,128)(2,1)}, f32[8,16,128]{2,1,0:T(8,128)}) custom-call(bf16[8,16,128]{2,1,0:T(8,128)(2,1)S(1)} %get-tuple-element.4.upd_ref, f32[8,16,128]{2,1,0:T(8,128)S(1)} %get-tuple-element.5.grad_ref), custom_call_target="tpu_custom_call" | custom-call | tf_op jit(solution)/shard_map/store_outputs/pallas_call | solution.py:357
